TPU v7x, 256 devices: a whole 4x4x8 slice. The times are simulated.
256 devices in a mesh: exp: 64 (over z, x, core), seq: 4 (over y).
Axes of the slice: x: 4, y: 4, z: 8, core: 2. Of those that a mesh axis runs over, the one named last changes fastest.
Arguments:
- layer_output_gradient: bfloat16 [2048, 7168], P(('exp', 'seq')), may hold values from -24 to 24
- residual_input: bfloat16 [2048, 7168], P(('exp', 'seq')), may hold values from -6 to 6
- norm_scale_vector: bfloat16 [7168], replicated, may hold values from 0.5 to 1.5
- chosen_expert_index: int32 [2048, 8], P(('exp', 'seq')), may hold values from 0 to 63, all different within a row; in each aligned block of 32 rows (0 to 31, 32 to 63, ...) at most 8 rows name the same one
- routing_gate_weight: bfloat16 [2048, 8], P(('exp', 'seq')), may hold values from 0.099609375 to 0.59765625
- expert_gate_weight: bfloat16 [64, 7168, 1024], P('exp', None, 'seq'), may hold values from -0.0625 to 0.0625
- expert_up_weight: bfloat16 [64, 7168, 1024], P('exp', None, 'seq'), may hold values from -0.0625 to 0.0625
- expert_down_weight: bfloat16 [64, 1024, 7168], P('exp', 'seq'), may hold values from -0.1875 to 0.1875
- stored_gate_state: bfloat16 [64, 512, 1024], P('exp', None, 'seq'), may hold values from -6 to 6
- stored_up_state: bfloat16 [64, 512, 1024], P('exp', None, 'seq'), may hold values from -6 to 6
- attention_output: bfloat16 [2048, 16384], P(('exp', 'seq')), may hold values from -24 to 24
- saved_adapter_latent: bfloat16 [2048, 32], P(('exp', 'seq')), may hold values from -0.109375 to 0.109375
- adapter_up_matrix: bfloat16 [32, 7168], replicated, may hold values from -0.00048828125 to 0.00048828125
Outputs:
- hidden_state_gradient: bfloat16 [2048, 7168], P(('exp', 'seq'))
- adapter_down_gradient: float32 [16384, 32], P(('exp', 'seq'))
- adapter_up_gradient_transposed: float32 [7168, 32], P(('exp', 'seq'))
Inputs may be any that keep to these rules, and one draw needn't show every extreme that they name: `chosen_expert_index`: each row names 8 different experts. In each aligned block of 32 rows (the tokens of one index of exp) no expert is named by more than 8 rows, and in some block some expert is named by exactly 8 rows.
All inputs are finite; a program needn't handle non-finite values.
Results may differ from a plain program's by a relative error of at most 0.015.
Values may be sent and summed in bfloat16 or wider, within the bound.
A program may use at most 128 MiB of HBM per device.

v0:
```python
import jax
import jax.numpy as jnp
from jax import lax
from jax.sharding import PartitionSpec as P

ADAPTER_SCALE = 2.0
NORM_EPS = 1e-06


def silu_parts(gate_val):
    sigmoid_val = jax.nn.sigmoid(gate_val)
    return (gate_val * sigmoid_val, sigmoid_val * (1.0 + gate_val * (1.0 - sigmoid_val)))


def contract_trailing(left, right):
    return lax.dot_general(
        left, right, (((1,), (1,)), ((), ())), preferred_element_type=jnp.float32
    )


def contract_leading(left, right):
    return lax.dot_general(
        left, right, (((0,), (0,)), ((), ())), preferred_element_type=jnp.float32
    )


def per_device(
    layer_output_gradient,
    residual_input,
    norm_scale_vector,
    chosen_expert_index,
    routing_gate_weight,
    expert_gate_weight,
    expert_up_weight,
    expert_down_weight,
    stored_gate_state,
    stored_up_state,
    attention_output,
    saved_adapter_latent,
    adapter_up_matrix,
):
    model_width = layer_output_gradient.shape[1]
    experts = lax.axis_size("exp") * expert_gate_weight.shape[0]
    capacity = stored_gate_state.shape[1] // experts
    group_grad, group_ids, group_weights = (
        lax.all_gather(layer_output_gradient, "seq", axis=0, tiled=True),
        lax.all_gather(chosen_expert_index, "seq", axis=0, tiled=True),
        lax.all_gather(routing_gate_weight, "seq", axis=0, tiled=True),
    )
    group_size = group_grad.shape[0]
    top_count = group_ids.shape[1]
    labels = jnp.arange(experts, dtype=jnp.int32)
    named_by = jnp.sum((group_ids[:, :, None] == labels[None, None, :]).astype(jnp.int32), axis=1)
    before = jnp.cumsum(named_by, axis=0) - named_by
    position = jnp.take_along_axis(before, group_ids, axis=1)
    slot_index = (group_ids * capacity + position).reshape(-1).astype(jnp.int32)
    token_ids = jnp.repeat(jnp.arange(group_size, dtype=jnp.int32), top_count)
    slot_owner = (
        jnp.full((experts * capacity,), group_size, jnp.int32).at[slot_index].set(token_ids)
    )
    padded = jnp.concatenate([group_grad, jnp.zeros((1, model_width), group_grad.dtype)], axis=0)
    outgoing = padded[slot_owner].reshape(experts, capacity, model_width)
    incoming = lax.all_to_all(outgoing, "exp", split_axis=0, concat_axis=0, tiled=True)
    slot_rows = incoming.reshape(-1, model_width)
    hidden_grad = contract_trailing(slot_rows, expert_down_weight[0])
    activation, silu_slope = silu_parts(stored_gate_state[0].astype(jnp.float32))
    gate_grad = (hidden_grad * stored_up_state[0].astype(jnp.float32) * silu_slope).astype(
        jnp.bfloat16
    )
    up_grad = (hidden_grad * activation).astype(jnp.bfloat16)
    partial_value = (
        contract_trailing(gate_grad, expert_gate_weight[0])
        + contract_trailing(up_grad, expert_up_weight[0])
    ).astype(jnp.bfloat16)
    sources = partial_value.shape[0] // capacity
    weights = group_weights.astype(jnp.float32)
    returned = lax.all_to_all(
        partial_value.reshape(sources, capacity, model_width),
        "exp",
        split_axis=0,
        concat_axis=0,
        tiled=True,
    )
    combine_returned = returned.reshape(experts * capacity, model_width)
    picked = combine_returned[slot_index].reshape(group_size, top_count, -1).astype(jnp.float32)
    combined = jnp.sum(picked * weights[:, :, None], axis=1)
    moe_grad = lax.psum_scatter(
        combined.astype(jnp.bfloat16), "seq", scatter_dimension=0, tiled=True
    ).astype(jnp.float32)
    residual = residual_input.astype(jnp.float32)
    inverse_rms = lax.rsqrt(jnp.mean(residual * residual, axis=1, keepdims=True) + NORM_EPS)
    scaled = norm_scale_vector.astype(jnp.float32)[None, :] * moe_grad
    inner_mean = jnp.mean(scaled * residual, axis=1, keepdims=True)
    hidden_state_gradient = (
        layer_output_gradient.astype(jnp.float32)
        + inverse_rms * scaled
        - residual * inner_mean * inverse_rms**3
    ).astype(jnp.bfloat16)
    adapter_latent_value = (
        ADAPTER_SCALE * contract_trailing(hidden_state_gradient, adapter_up_matrix)
    ).astype(jnp.bfloat16)
    down_contribution = contract_leading(attention_output, adapter_latent_value)
    up_contribution = ADAPTER_SCALE * contract_leading(hidden_state_gradient, saved_adapter_latent)
    complete_down_matrix, complete_up_matrix = lax.psum(
        (down_contribution, up_contribution), ("exp", "seq")
    )
    slot_member = lax.axis_index(("exp", "seq"))
    members = lax.axis_size(("exp", "seq"))
    down_projection_rows = complete_down_matrix.shape[0] // members
    up_projection_rows = complete_up_matrix.shape[0] // members
    adapter_down_gradient = lax.dynamic_slice_in_dim(
        complete_down_matrix, slot_member * down_projection_rows, down_projection_rows, 0
    )
    adapter_up_gradient_transposed = lax.dynamic_slice_in_dim(
        complete_up_matrix, slot_member * up_projection_rows, up_projection_rows, 0
    )
    return (hidden_state_gradient, adapter_down_gradient, adapter_up_gradient_transposed)


def solution(mesh):
    return jax.shard_map(
        per_device,
        mesh=mesh,
        in_specs=(
            P(("exp", "seq"), None),
            P(("exp", "seq"), None),
            P(),
            P(("exp", "seq"), None),
            P(("exp", "seq"), None),
            P("exp", None, "seq"),
            P("exp", None, "seq"),
            P("exp", "seq", None),
            P("exp", None, "seq"),
            P("exp", None, "seq"),
            P(("exp", "seq"), None),
            P(("exp", "seq"), None),
            P(),
        ),
        out_specs=(P(("exp", "seq"), None), P(("exp", "seq"), None), P(("exp", "seq"), None)),
        check_vma=False,
    )
```

profile of v0, /device:TPU:2, one launch (start us, length us, event | category | flops | bytes accessed | tf_op | source)
XLA Modules:
  0.0 736.5 jit_solution(16224991714569872756)
XLA Ops:
  7.2 0.0 copy-start
  7.2 12.7 %all_gather.10 = s32[32,8]{1,0:T(8,128)S(1)} all-gather(s32[8,8]{1,0:T(8,128)} %param.16), channel_id=1, replica_groups=mesh['exp'=64,'seq'=4] {'seq'}, dimensions={0}, use_global_device_ids=true | all-gather | bytes 1280 | tf_op jit(solution)/shard_map/all_gather | solution.py:47
  19.9 0.1 convert_reduce_fusion
  20.0 0.1 reduce_window_sum.11
  20.1 0.1 reshape.115
  20.2 0.0 copy-start.6
  20.2 1.9 gather_fusion.2
  22.2 0.1 reshape.118
  22.3 0.1 reshape.90
  22.4 0.1 reshape.125
  22.5 1.4 scatter_custom_fusion
  23.9 0.0 copy-done.6
  23.9 12.7 %all_gather.9 = bf16[32,7168]{1,0:T(8,128)(2,1)S(1)} all-gather(bf16[8,7168]{1,0:T(8,128)(2,1)S(1)} %copy-done.6), channel_id=1, replica_groups=mesh['exp'=64,'seq'=4] {'seq'}, dimensions={0}, use_global_device_ids=true | all-gather | bytes 573440 | tf_op jit(solution)/shard_map/all_gather | solution.py:46
  36.6 7.1 gather_fusion
  43.6 0.0 copy-start.12
  43.6 175.9 %all_to_all.10 = bf16[64,8,7168]{2,1,0:T(8,128)(2,1)S(1)} all-to-all(bf16[64,8,7168]{2,1,0:T(8,128)(2,1)} %bitcast.47), channel_id=1, replica_groups=mesh['exp'=64,'seq'=4] {'exp'}, dimensions={0} | all-to-all | bytes 14680064 | tf_op jit(solution)/shard_map/all_to_all | solution.py:63
  219.5 0.0 copy-done.12
  219.5 0.0 copy-start.1
  219.6 0.0 copy-start.3
  219.6 0.0 copy-start.7
  219.6 2.1 fusion.2
  221.7 0.0 copy-done.1
  221.7 0.0 copy-done.3
  221.7 0.0 copy-done.7
  221.7 0.0 copy-start.2
  221.7 7.4 %fusion.5 = f32[512,7168]{1,0:T(8,128)} fusion(bf16[1,7168,256]{2,1,0:T(8,128)(2,1)S(1)} %copy-done.1, f32[512,256]{1,0:T(8,128)S(1)} %fusion.2, bf16[1,512,256]{2,1,0:T(8,128)(2,1)S(1)} %copy-done.7, bf16[1,512,256]{2,1,0:T(8,128)(2,1)S(1)} %copy-done.3), kind=kOutput, calls=%fused_computation.13 | convolution fusion | flops 1880621056 | bytes 19398656 | tf_op jit(solution)/shard_map/dot_general | solution.py:16
  229.1 0.0 copy-done.2
  229.1 10.3 %fusion = bf16[64,8,7168]{2,1,0:T(8,128)(2,1)} fusion(f32[512,7168]{1,0:T(8,128)} %fusion.5, bf16[1,7168,256]{2,1,0:T(8,128)(2,1)S(1)} %copy-done.2, f32[512,256]{1,0:T(8,128)S(1)} %fusion.2, bf16[1,512,256]{2,1,0:T(8,128)(2,1)S(1)} %copy-done.3), kind=kOutput, calls=%fused_computation.6 | convolution fusion | flops 1887305728 | bytes 26476544 | tf_op jit(solution)/shard_map/dot_general | solution.py:16
  239.4 0.0 copy-start.11
  239.4 6.0 all-to-all-start.1
  245.4 0.0 reduce-scatter.2.cloned.1.call-start
  245.4 0.0 copy-done.11
  245.4 10.6 %all_gather.11 = bf16[32,8]{1,0:T(8,128)(2,1)S(1)} all-gather(bf16[8,8]{1,0:T(8,128)(2,1)S(1)} %copy-done.11), channel_id=1, replica_groups=mesh['exp'=64,'seq'=4] {'seq'}, dimensions={0}, use_global_device_ids=true | all-gather | bytes 640 | tf_op jit(solution)/shard_map/all_gather | solution.py:48
  256.0 151.7 %all-to-all-done.1 = bf16[64,8,7168]{2,1,0:T(8,128)(2,1)} async-done(((bf16[64,8,7168]{2,1,0:T(8,128)(2,1)}), bf16[64,8,7168]{2,1,0:T(8,128)(2,1)}, u32[]{:S(2)}, u32[]{:S(2)}) %all-to-all-start.1) | async-done | bytes 7340064 | tf_op jit(solution)/shard_map/all_to_all | solution.py:77
  407.7 12.1 %gather_fusion.1 = bf16[256,7168]{1,0:T(8,128)(2,1)} fusion(bf16[512,7168]{1,0:T(8,128)(2,1)} %bitcast.11, s32[1024]{0:T(1024)S(1)} %pad_clamp_fusion), kind=kCustom, calls=%fused_computation.1 | custom fusion | bytes 7341056 | tf_op jit(solution)/shard_map/gather | solution.py:85
  419.9 0.0 copy-start.9
  419.9 0.0 copy-start.5
  419.9 0.0 copy-start.10
  419.9 0.0 copy-start.8
  419.9 5.5 fusion.1
  425.3 0.0 reduce-scatter.2.cloned.1.call-update
  425.4 0.0 all-reduce.4.cloned.1.call-start
  425.4 0.0 copy-done.9
  425.4 21.3 %reduce-scatter.2.cloned.1.call-done = bf16[8,7168]{1,0:T(8,128)(2,1)} async-done(((bf16[32,7168]{1,0:T(8,128)(2,1)}), bf16[8,7168]{1,0:T(8,128)(2,1)}) %reduce-scatter.2.cloned.1.call-update) | async-done | bytes 114704 | tf_op jit(solution)/shard_map/reduce_scatter | solution.py:87
  446.7 0.0 copy-done.5
  446.7 1.1 fusion.26
  447.8 1.0 fusion.29
  448.9 0.0 copy-done.10
  448.9 0.0 copy-start.4
  448.9 2.7 convolution_multiply_fusion
  451.6 0.0 copy-done
  451.6 0.0 copy-done.8
  451.6 2.3 convolution_bitcast_fusion
  453.8 0.0 all-reduce.4.cloned.1.call-update
  453.9 0.0 copy-done.4
  453.9 273.0 %all-reduce.4.cloned.1.call-done = (f32[16384,32]{0,1:T(8,128)}, f32[7168,32]{1,0:T(8,128)}) async-done(((f32[16384,32]{0,1:T(8,128)}, f32[7168,32]{1,0:T(8,128)}), (f32[16384,32]{0,1:T(8,128)}, f32[7168,32]{1,0:T(8,128)})) %all-reduce.4.cloned.1.call-update) | async-done | bytes 3014672 | tf_op jit(solution)/shard_map/psum | solution.py:104
  726.9 1.3 constant_dynamic-slice_fusion
  728.3 1.4 constant_dynamic-slice_fusion.1
  (12 shorter events, 0.1 us)
Async XLA Ops:
  7.2 444.4 %copy-start = (bf16[32,7168]{1,0:T(8,128)(2,1)S(1)}, bf16[32,7168]{1,0:T(8,128)(2,1)}, u32[]{:S(2)}) copy-start(bf16[32,7168]{1,0:T(8,128)(2,1)} %param.25) | copy-start | bytes 1376260
  20.2 3.7 copy-start.6
  43.6 175.9 %copy-start.12 = (bf16[1,256,7168]{2,1,0:T(8,128)(2,1)S(1)}, bf16[1,256,7168]{2,1,0:T(8,128)(2,1)}, u32[]{:S(2)}) copy-start(bf16[1,256,7168]{2,1,0:T(8,128)(2,1)} %param.20) | copy-start | bytes 11010052
  219.5 2.1 copy-start.1
  219.6 2.1 copy-start.3
  219.6 2.1 copy-start.7
  221.7 7.4 %copy-start.2 = (bf16[1,7168,256]{2,1,0:T(8,128)(2,1)S(1)}, bf16[1,7168,256]{2,1,0:T(8,128)(2,1)}, u32[]{:S(2)}) copy-start(bf16[1,7168,256]{2,1,0:T(8,128)(2,1)} %param.19) | copy-start | bytes 11010052
  239.4 6.0 copy-start.11
  239.4 168.3 %all-to-all-start.1 = ((bf16[64,8,7168]{2,1,0:T(8,128)(2,1)}), bf16[64,8,7168]{2,1,0:T(8,128)(2,1)}, u32[]{:S(2)}, u32[]{:S(2)}) async-start(bf16[64,8,7168]{2,1,0:T(8,128)(2,1)} %fusion), calls=%async_computation.1 | async-start | bytes 14680064 | tf_op jit(solution)/shard_map/all_to_all | solution.py:77
  245.4 201.3 %reduce-scatter.2.cloned.1.call-start = ((), (), s32[]{:S(2)}) async-start(), calls=%async_computation.3 | async-start | bytes 573440 | tf_op jit(solution)/shard_map/reduce_scatter | solution.py:87
  419.9 5.6 copy-start.9
  419.9 26.9 %copy-start.5 = (bf16[8,7168]{1,0:T(8,128)(2,1)S(1)}, bf16[8,7168]{1,0:T(8,128)(2,1)}, u32[]{:S(2)}) copy-start(bf16[8,7168]{1,0:T(8,128)(2,1)} %param.14) | copy-start | bytes 344068
  419.9 29.0 %copy-start.10 = (bf16[8,32]{1,0:T(8,128)(2,1)S(1)}, bf16[8,32]{1,0:T(8,128)(2,1)}, u32[]{:S(2)}) copy-start(bf16[8,32]{1,0:T(8,128)(2,1)} %param.24) | copy-start | bytes 1540
  419.9 31.7 %copy-start.8 = (bf16[8,16384]{1,0:T(8,128)(2,1)S(1)}, bf16[8,16384]{1,0:T(8,128)(2,1)}, u32[]{:S(2)}) copy-start(bf16[8,16384]{1,0:T(8,128)(2,1)} %param.23) | copy-start | bytes 786436
  425.4 301.6 %all-reduce.4.cloned.1.call-start = ((), (), s32[]{:S(2)}) async-start(), calls=%async_computation.4 | async-start | bytes 11534336 | tf_op jit(solution)/shard_map/psum | solution.py:104
  448.9 5.0 copy-start.4
Sparse Core Ops, SparseCore 0:
  425.5 21.1 reduce-scatter.1
  454.0 272.8 all-reduce.3
where the time goes:
time: 737 us; the launch traced here: 736 us
  waiting for transfers between devices  446 us (61%)
  blocking collectives  212 us (29%)
  local copies, waits for them, and re-layouts  25.7 us (3%)
  matrix products  24.7 us (3%)
  between operations  14.3 us (2%)
  other arithmetic  7.84 us (1%)
    psum x1, waiting for transfers between devices, per_device(): lax.psum((down_contribution, up_contribution), ('exp', 'seq'))  273 us
    all_to_all x1, blocking collectives, per_device(): lax.all_to_all(outgoing, 'exp', split_axis=0, concat_axis=0, tiled=True)  176 us
    all_to_all x1, waiting for transfers between devices, per_device(): lax.all_to_all(partial_value.reshape(sources, capacity, model_width), 'ex...  152 us
    reduce_scatter x1, waiting for transfers between devices, per_device(): lax.psum_scatter(combined.astype(jnp.bfloat16), 'seq', scatter_dimension=...  21.3 us
    dot_general x3, matrix products, contract_trailing(): lax.dot_general(left, right, (((1,), (1,)), ((), ())), preferred_element_...  19.8 us
  transfers between devices with their start and end apart: 3, of which 3 were waited for; matrix products, arithmetic and copies ran while one was open for 0% of the time, Pallas kernels for 0%

commit v1 on v0

--- a/solution.py
+++ b/solution.py
@@ -5,6 +5,12 @@
 
 ADAPTER_SCALE = 2.0
 NORM_EPS = 1e-06
+
+
+def fill_case_now(array_here):
+    for u in ("seq", "exp"):
+        array_here = jax.lax.psum(array_here, axis_name=u)
+    return array_here
 
 
 def silu_parts(gate_val):
@@ -101,9 +107,7 @@
     ).astype(jnp.bfloat16)
     down_contribution = contract_leading(attention_output, adapter_latent_value)
     up_contribution = ADAPTER_SCALE * contract_leading(hidden_state_gradient, saved_adapter_latent)
-    complete_down_matrix, complete_up_matrix = lax.psum(
-        (down_contribution, up_contribution), ("exp", "seq")
-    )
+    complete_down_matrix, complete_up_matrix = fill_case_now((down_contribution, up_contribution))
     slot_member = lax.axis_index(("exp", "seq"))
     members = lax.axis_size(("exp", "seq"))
     down_projection_rows = complete_down_matrix.shape[0] // members

time: 737 us -> 791 us (1.073)
  waiting for transfers between devices: 446 us -> 500 us
    psum x1 -> x2, waiting for transfers between devices: 273 us -> 327 us  [fill_case_now(): array_here = jax.lax.psum(array_here, axis_name=u)]
  transfers between devices with their start and end apart: 3 -> 4, of which waited for: 3 -> 4; matrix products, arithmetic and copies ran while one was open for 0% -> 0% of each run, Pallas kernels for 0% -> 0%
where the time goes in v1:
time: 791 us; the launch traced here: 790 us
  waiting for transfers between devices  500 us (63%)
  blocking collectives  212 us (27%)
  local copies, waits for them, and re-layouts  25.7 us (3%)
  matrix products  24.7 us (3%)
  between operations  14 us (2%)
    psum x2, waiting for transfers between devices, fill_case_now(): array_here = jax.lax.psum(array_here, axis_name=u)  327 us
    all_to_all x1, blocking collectives, per_device(): lax.all_to_all(outgoing, 'exp', split_axis=0, concat_axis=0, tiled=True)  176 us
    all_to_all x1, waiting for transfers between devices, per_device(): lax.all_to_all(partial_value.reshape(sources, capacity, model_width), 'ex...  152 us
    reduce_scatter x1, waiting for transfers between devices, per_device(): lax.psum_scatter(combined.astype(jnp.bfloat16), 'seq', scatter_dimension=...  21.3 us
    dot_general x3, matrix products, contract_trailing(): lax.dot_general(left, right, (((1,), (1,)), ((), ())), preferred_element_...  19.8 us
  transfers between devices with their start and end apart: 4, of which 4 were waited for; matrix products, arithmetic and copies ran while one was open for 0% of the time, Pallas kernels for 0%

profile of v1, /device:TPU:2, one launch (start us, length us, event | category | flops | bytes accessed | tf_op | source)
XLA Modules:
  0.0 789.9 jit_solution(16030901956927473295)
XLA Ops:
  7.2 0.0 copy-start
  7.2 12.7 %all_gather.10 = s32[32,8]{1,0:T(8,128)S(1)} all-gather(s32[8,8]{1,0:T(8,128)} %param.16), channel_id=1, replica_groups=mesh['exp'=64,'seq'=4] {'seq'}, dimensions={0}, use_global_device_ids=true | all-gather | bytes 1280 | tf_op jit(solution)/shard_map/all_gather | solution.py:53
  19.9 0.1 convert_reduce_fusion
  20.0 0.1 reduce_window_sum.11
  20.1 0.1 reshape.115
  20.2 0.0 copy-start.6
  20.2 1.9 gather_fusion.2
  22.2 0.1 reshape.118
  22.3 0.1 reshape.90
  22.4 0.1 reshape.125
  22.5 1.4 scatter_custom_fusion
  23.9 0.0 copy-done.6
  23.9 12.7 %all_gather.9 = bf16[32,7168]{1,0:T(8,128)(2,1)S(1)} all-gather(bf16[8,7168]{1,0:T(8,128)(2,1)S(1)} %copy-done.6), channel_id=1, replica_groups=mesh['exp'=64,'seq'=4] {'seq'}, dimensions={0}, use_global_device_ids=true | all-gather | bytes 573440 | tf_op jit(solution)/shard_map/all_gather | solution.py:52
  36.6 7.1 gather_fusion
  43.7 0.0 copy-start.12
  43.7 175.9 %all_to_all.10 = bf16[64,8,7168]{2,1,0:T(8,128)(2,1)S(1)} all-to-all(bf16[64,8,7168]{2,1,0:T(8,128)(2,1)} %bitcast.47), channel_id=1, replica_groups=mesh['exp'=64,'seq'=4] {'exp'}, dimensions={0} | all-to-all | bytes 14680064 | tf_op jit(solution)/shard_map/all_to_all | solution.py:69
  219.6 0.0 copy-done.12
  219.6 0.0 copy-start.1
  219.6 0.0 copy-start.3
  219.6 0.0 copy-start.7
  219.6 2.1 fusion.2
  221.7 0.0 copy-done.1
  221.7 0.0 copy-done.3
  221.7 0.0 copy-done.7
  221.7 0.0 copy-start.2
  221.7 7.4 fusion.5
  229.2 0.0 copy-done.2
  229.2 10.3 %fusion = bf16[64,8,7168]{2,1,0:T(8,128)(2,1)} fusion(f32[512,7168]{1,0:T(8,128)} %fusion.5, bf16[1,7168,256]{2,1,0:T(8,128)(2,1)S(1)} %copy-done.2, f32[512,256]{1,0:T(8,128)S(1)} %fusion.2, bf16[1,512,256]{2,1,0:T(8,128)(2,1)S(1)} %copy-done.3), kind=kOutput, calls=%fused_computation.6 | convolution fusion | flops 1887305728 | bytes 26476544 | tf_op jit(solution)/shard_map/dot_general | solution.py:22
  239.4 0.0 copy-start.11
  239.4 6.0 all-to-all-start.1
  245.4 0.0 reduce-scatter.2.cloned.1.call-start
  245.4 0.0 copy-done.11
  245.4 10.6 %all_gather.11 = bf16[32,8]{1,0:T(8,128)(2,1)S(1)} all-gather(bf16[8,8]{1,0:T(8,128)(2,1)S(1)} %copy-done.11), channel_id=1, replica_groups=mesh['exp'=64,'seq'=4] {'seq'}, dimensions={0}, use_global_device_ids=true | all-gather | bytes 640 | tf_op jit(solution)/shard_map/all_gather | solution.py:54
  256.0 151.7 %all-to-all-done.1 = bf16[64,8,7168]{2,1,0:T(8,128)(2,1)} async-done(((bf16[64,8,7168]{2,1,0:T(8,128)(2,1)}), bf16[64,8,7168]{2,1,0:T(8,128)(2,1)}, u32[]{:S(2)}, u32[]{:S(2)}) %all-to-all-start.1) | async-done | bytes 7340064 | tf_op jit(solution)/shard_map/all_to_all | solution.py:83
  407.7 12.1 %gather_fusion.1 = bf16[256,7168]{1,0:T(8,128)(2,1)} fusion(bf16[512,7168]{1,0:T(8,128)(2,1)} %bitcast.11, s32[1024]{0:T(1024)S(1)} %pad_clamp_fusion), kind=kCustom, calls=%fused_computation.1 | custom fusion | bytes 7341056 | tf_op jit(solution)/shard_map/gather | solution.py:91
  419.9 0.0 copy-start.9
  419.9 0.0 copy-start.5
  419.9 0.0 copy-start.10
  419.9 0.0 copy-start.8
  419.9 5.5 fusion.1
  425.3 0.0 reduce-scatter.2.cloned.1.call-update
  425.4 0.0 all-reduce.8.cloned.1.call-start
  425.4 0.0 copy-done.9
  425.4 21.3 %reduce-scatter.2.cloned.1.call-done = bf16[8,7168]{1,0:T(8,128)(2,1)} async-done(((bf16[32,7168]{1,0:T(8,128)(2,1)}), bf16[8,7168]{1,0:T(8,128)(2,1)}) %reduce-scatter.2.cloned.1.call-update) | async-done | bytes 114704 | tf_op jit(solution)/shard_map/reduce_scatter | solution.py:93
  446.7 0.0 copy-done.5
  446.7 1.1 fusion.26
  447.8 1.0 fusion.29
  448.9 0.0 copy-done.10
  448.9 0.0 copy-start.4
  448.9 2.7 convolution_multiply_fusion
  451.6 0.0 copy-done
  451.6 0.0 copy-done.8
  451.6 2.2 convolution_bitcast_fusion
  453.8 0.0 all-reduce.8.cloned.1.call-update
  453.9 0.0 copy-done.4
  453.9 0.0 all-reduce.6.cloned.1.call-start
  453.9 123.5 %all-reduce.8.cloned.1.call-done = (f32[16384,32]{0,1:T(8,128)}, f32[7168,32]{1,0:T(8,128)}) async-done(((f32[16384,32]{0,1:T(8,128)}, f32[7168,32]{1,0:T(8,128)}), (f32[16384,32]{0,1:T(8,128)}, f32[7168,32]{1,0:T(8,128)})) %all-reduce.8.cloned.1.call-update) | async-done | bytes 3014672 | tf_op jit(solution)/shard_map/psum | solution.py:12
  577.4 0.0 all-reduce.6.cloned.1.call-update
  577.5 203.1 %all-reduce.6.cloned.1.call-done = (f32[16384,32]{0,1:T(8,128)}, f32[7168,32]{1,0:T(8,128)}) async-done(((f32[16384,32]{0,1:T(8,128)}, f32[7168,32]{1,0:T(8,128)}), (f32[16384,32]{0,1:T(8,128)}, f32[7168,32]{1,0:T(8,128)})) %all-reduce.6.cloned.1.call-update) | async-done | bytes 3014672 | tf_op jit(solution)/shard_map/psum | solution.py:12
  780.6 1.3 constant_dynamic-slice_fusion
  781.9 1.4 constant_dynamic-slice_fusion.1
  (12 shorter events, 0.1 us)
Async XLA Ops:
  7.2 444.4 %copy-start = (bf16[32,7168]{1,0:T(8,128)(2,1)S(1)}, bf16[32,7168]{1,0:T(8,128)(2,1)}, u32[]{:S(2)}) copy-start(bf16[32,7168]{1,0:T(8,128)(2,1)} %param.25) | copy-start | bytes 1376260
  20.2 3.7 copy-start.6
  43.7 175.9 %copy-start.12 = (bf16[1,256,7168]{2,1,0:T(8,128)(2,1)S(1)}, bf16[1,256,7168]{2,1,0:T(8,128)(2,1)}, u32[]{:S(2)}) copy-start(bf16[1,256,7168]{2,1,0:T(8,128)(2,1)} %param.20) | copy-start | bytes 11010052
  219.6 2.1 copy-start.1
  219.6 2.1 copy-start.3
  219.6 2.1 copy-start.7
  221.7 7.5 copy-start.2
  239.4 6.0 copy-start.11
  239.4 168.3 %all-to-all-start.1 = ((bf16[64,8,7168]{2,1,0:T(8,128)(2,1)}), bf16[64,8,7168]{2,1,0:T(8,128)(2,1)}, u32[]{:S(2)}, u32[]{:S(2)}) async-start(bf16[64,8,7168]{2,1,0:T(8,128)(2,1)} %fusion), calls=%async_computation.1 | async-start | bytes 14680064 | tf_op jit(solution)/shard_map/all_to_all | solution.py:83
  245.4 201.3 %reduce-scatter.2.cloned.1.call-start = ((), (), s32[]{:S(2)}) async-start(), calls=%async_computation.3 | async-start | bytes 573440 | tf_op jit(solution)/shard_map/reduce_scatter | solution.py:93
  419.9 5.5 copy-start.9
  419.9 26.9 %copy-start.5 = (bf16[8,7168]{1,0:T(8,128)(2,1)S(1)}, bf16[8,7168]{1,0:T(8,128)(2,1)}, u32[]{:S(2)}) copy-start(bf16[8,7168]{1,0:T(8,128)(2,1)} %param.14) | copy-start | bytes 344068
  419.9 29.0 %copy-start.10 = (bf16[8,32]{1,0:T(8,128)(2,1)S(1)}, bf16[8,32]{1,0:T(8,128)(2,1)}, u32[]{:S(2)}) copy-start(bf16[8,32]{1,0:T(8,128)(2,1)} %param.24) | copy-start | bytes 1540
  419.9 31.7 %copy-start.8 = (bf16[8,16384]{1,0:T(8,128)(2,1)S(1)}, bf16[8,16384]{1,0:T(8,128)(2,1)}, u32[]{:S(2)}) copy-start(bf16[8,16384]{1,0:T(8,128)(2,1)} %param.23) | copy-start | bytes 786436
  425.4 152.1 %all-reduce.8.cloned.1.call-start = ((), (), s32[]{:S(2)}) async-start(), calls=%async_computation.5 | async-start | bytes 11534336 | tf_op jit(solution)/shard_map/psum | solution.py:12
  448.9 5.0 copy-start.4
  453.9 326.7 %all-reduce.6.cloned.1.call-start = ((), (), s32[]{:S(2)}) async-start(), calls=%async_computation.4 | async-start | bytes 11534336 | tf_op jit(solution)/shard_map/psum | solution.py:12
Sparse Core Ops, SparseCore 0:
  425.5 21.1 reduce-scatter.1
  454.0 123.3 all-reduce.7
  581.6 198.9 all-reduce.5
